TPU v7x, 32 devices: a whole 2x2x4 slice. The times are simulated.
32 devices in a mesh: dp: 4 (over y, x), fsdp: 8 (over z, core).
Axes of the slice: x: 2, y: 2, z: 4, core: 2. Of those that a mesh axis runs over, the one named last changes fastest.
Arguments:
- inputs: bfloat16 [512, 16384], P('dp', 'fsdp'), may hold values from -140 to 140
- norm_gain_vector: bfloat16 [16384], P('fsdp'), may hold values from 0.5 to 1.5
- weight: bfloat16 [16384, 16384], P(None, 'fsdp'), may hold values from -0.046875 to 0.046875
- down_adapters: bfloat16 [16384, 16, 32], P('fsdp'), may hold values from -0.046875 to 0.046875
- up_adapters: bfloat16 [16, 32, 16384], P(None, None, 'fsdp'), may hold values from -1 to 1
- tenant: int32 [512], P('dp'), may hold values from 0 to 15
- tenant_slot_index: int32 [16], replicated, may hold values from 0 to 31, as said below
- live_row_count: int32 [4], P('dp'), may hold values from 1 to 128, 320 in all
- cotangent: bfloat16 [512, 16384], P('dp', 'fsdp'), may hold values from -6 to 6
- down_row_factor: float32 [32, 16384], P('dp', 'fsdp'), may hold values from 300 to 30000
- down_column_factor: float32 [32, 32], P('dp'), may hold values from 300 to 30000
- up_row_factor: float32 [32, 32], P('dp'), may hold values from 0.5 to 50
- up_column_factor: float32 [32, 16384], P('dp', 'fsdp'), may hold values from 0.5 to 50
Outputs:
- projected: bfloat16 [512, 16384], P('dp', 'fsdp')
- normed_gradient_transposed: bfloat16 [16384, 512], P('fsdp', 'dp')
- update_a: float32 [32, 16384, 32], P('dp', 'fsdp')
- update_b: float32 [32, 32, 16384], P('dp', None, 'fsdp')
- row_a_new: float32 [32, 16384], P('dp', 'fsdp')
- col_a_new: float32 [32, 32], P('dp')
- row_b_new: float32 [32, 32], P('dp')
- col_b_new: float32 [32, 16384], P('dp', 'fsdp')
Inputs may be any that keep to these rules, and one draw needn't show every extreme that they name: Distinct slots; tenant t's optimizer state is in slot tenant_slot_index[t], owned by data group tenant_slot_index[t] // 8; every group owns at most 8 tenants and some group owns exactly 8. The first live_row_count[g] rows of data group g are live; some group has all 128 live; the counts sum to 320.
All inputs are finite; a program needn't handle non-finite values.
Results may differ from a plain program's by a relative error of at most 0.0095.
Values may be sent and summed in bfloat16 or wider, within the bound.
A program may use at most 192 MiB of HBM per device.

v0:
```python
import jax
import jax.numpy as jnp
from jax import lax
from jax.sharding import PartitionSpec as P

ADAPTER_SCALE = 0.5
BETA_TWO = 0.9
SQ_EPS = 1e-30
RMS_EPS = 1e-05


def on_device(
    inputs,
    norm_gain_vector,
    weight,
    down_adapters,
    up_adapters,
    tenant,
    tenant_slot_index,
    live_row_count,
    cotangent,
    down_row_factor,
    down_column_factor,
    up_row_factor,
    up_column_factor,
):
    highest_precision = lax.Precision.HIGHEST
    rows, shard_local_width = inputs.shape
    full_width = weight.shape[0]
    tenant_index = down_adapters.shape[1]
    device_rank = down_adapters.shape[2]
    contract_last = (((1,), (1,)), ((), ()))
    contract_first = (((0,), (0,)), ((), ()))
    local_f = inputs.astype(jnp.float32)
    power = lax.psum(jnp.sum(local_f * local_f, axis=1, keepdims=True), "fsdp")
    scale = lax.rsqrt(power / full_width + RMS_EPS)
    normalized_input = (local_f * scale * norm_gain_vector.astype(jnp.float32)).astype(jnp.bfloat16)
    weight_rows = weight
    frozen_output = jnp.dot(
        lax.all_gather(normalized_input, "fsdp", axis=1, tiled=True),
        weight_rows,
        preferred_element_type=jnp.float32,
    )
    pick = tenant[:, None] == lax.iota(jnp.int32, tenant_index)[None, :]
    pick_b = pick.astype(jnp.bfloat16)
    pick_f = pick.astype(jnp.float32)
    down_flattened = down_adapters.reshape(shard_local_width, tenant_index * device_rank)
    up_flattened = up_adapters.reshape(tenant_index * device_rank, up_adapters.shape[2])
    inner_all = jnp.dot(normalized_input, down_flattened, preferred_element_type=jnp.float32)
    inner_part = jnp.sum(
        inner_all.reshape(rows, tenant_index, device_rank) * pick_f[:, :, None], axis=1
    )
    inner = lax.psum(inner_part, "fsdp")
    spread_rows = (inner.astype(jnp.bfloat16)[:, None, :] * pick_b[:, :, None]).reshape(
        rows, tenant_index * device_rank
    )
    adapted_output = jnp.dot(spread_rows, up_flattened, preferred_element_type=jnp.float32)
    projected = (frozen_output + ADAPTER_SCALE * adapted_output).astype(jnp.bfloat16)
    live = lax.iota(jnp.int32, rows) < live_row_count[0]
    output_gradient = jnp.where(live[:, None], cotangent, jnp.zeros_like(cotangent))
    back_all = lax.dot_general(
        output_gradient, up_flattened, contract_last, preferred_element_type=jnp.float32
    )
    back_part = jnp.sum(
        back_all.reshape(rows, tenant_index, device_rank) * pick_f[:, :, None], axis=1
    )
    back = lax.psum(back_part, "fsdp")
    backward_spread_rows = (back.astype(jnp.bfloat16)[:, None, :] * pick_b[:, :, None]).reshape(
        rows, tenant_index * device_rank
    )
    weight_rows = weight
    frozen_input_gradient = lax.psum_scatter(
        lax.dot_general(
            weight_rows, output_gradient, contract_last, preferred_element_type=jnp.float32
        ),
        "fsdp",
        scatter_dimension=0,
        tiled=True,
    )
    adapter_input_gradient = lax.dot_general(
        down_flattened, backward_spread_rows, contract_last, preferred_element_type=jnp.float32
    )
    normed_gradient_transposed = (
        frozen_input_gradient + ADAPTER_SCALE * adapter_input_gradient
    ).astype(jnp.bfloat16)
    down_gradient = (
        ADAPTER_SCALE
        * lax.dot_general(
            normalized_input,
            backward_spread_rows,
            contract_first,
            preferred_element_type=jnp.float32,
        )
    ).reshape(shard_local_width, tenant_index, device_rank)
    up_gradient = (
        ADAPTER_SCALE
        * lax.dot_general(
            spread_rows, output_gradient, contract_first, preferred_element_type=jnp.float32
        )
    ).reshape(tenant_index, device_rank, output_gradient.shape[1])
    owned = down_row_factor.shape[0]
    summed_a, summed_b = (
        lax.psum(down_gradient.astype(jnp.bfloat16), "dp").astype(jnp.float32),
        lax.psum(up_gradient.astype(jnp.bfloat16), "dp").astype(jnp.float32),
    )
    mine = lax.iota(jnp.int32, owned) + lax.axis_index("dp") * owned
    owner_routing = (tenant_slot_index[None, :] == mine[:, None]).astype(jnp.float32)
    ga = jnp.einsum("st,ftr->sfr", owner_routing, summed_a, precision=highest_precision)
    gb = jnp.einsum("ho,oxk->hxk", owner_routing, summed_b, precision=highest_precision)
    sq_a = ga * ga + SQ_EPS
    sq_b = gb * gb + SQ_EPS
    row_a_new = BETA_TWO * down_row_factor + (1.0 - BETA_TWO) * (
        jnp.sum(sq_a, axis=2) / device_rank
    )
    col_b_new = BETA_TWO * up_column_factor + (1.0 - BETA_TWO) * (
        jnp.sum(sq_b, axis=1) / device_rank
    )
    col_sum, rowb_sum, meana_sum = lax.psum(
        (jnp.sum(sq_a, axis=1), jnp.sum(sq_b, axis=2), jnp.sum(row_a_new, axis=1)), "fsdp"
    )
    col_a_new = BETA_TWO * down_column_factor + (1.0 - BETA_TWO) * (col_sum / full_width)
    row_b_new = BETA_TWO * up_row_factor + (1.0 - BETA_TWO) * (rowb_sum / full_width)
    mean_a = meana_sum / full_width
    mean_b = jnp.sum(row_b_new, axis=1) / device_rank
    update_a = ga * lax.rsqrt(row_a_new[:, :, None] * col_a_new[:, None, :] / mean_a[:, None, None])
    update_b = gb * lax.rsqrt(row_b_new[:, :, None] * col_b_new[:, None, :] / mean_b[:, None, None])
    return (
        projected,
        normed_gradient_transposed,
        update_a,
        update_b,
        row_a_new,
        col_a_new,
        row_b_new,
        col_b_new,
    )


def solution(mesh):
    return jax.shard_map(
        on_device,
        mesh=mesh,
        in_specs=(
            P("dp", "fsdp"),
            P("fsdp"),
            P(None, "fsdp"),
            P("fsdp", None, None),
            P(None, None, "fsdp"),
            P("dp"),
            P(),
            P("dp"),
            P("dp", "fsdp"),
            P("dp", "fsdp"),
            P("dp", None),
            P("dp", None),
            P("dp", "fsdp"),
        ),
        out_specs=(
            P("dp", "fsdp"),
            P("fsdp", "dp"),
            P("dp", "fsdp", None),
            P("dp", None, "fsdp"),
            P("dp", "fsdp"),
            P("dp", None),
            P("dp", None),
            P("dp", "fsdp"),
        ),
        check_vma=False,
    )
```

profile of v0, /device:TPU:0, one launch (start us, length us, event | category | flops | bytes accessed | tf_op | source)
XLA Modules:
  0.0 251.9 jit_solution(4745225238941765912)
XLA Ops:
  8.1 0.8 convert_element_type.51
  8.9 1.3 fusion.20
  10.2 18.1 %psum.56 = f32[128,1]{0,1:T(1,128)S(1)} all-reduce(f32[128,1]{0,1:T(1,128)S(1)} %bitcast.76), channel_id=1, replica_groups=mesh['dp'=4,'fsdp'=8] {'fsdp'}, use_global_device_ids=true, to_apply=%region_1.0 | all-reduce | flops 128 | bytes 1024 | tf_op jit(solution)/shard_map/psum | solution.py:35
  28.3 0.7 fusion.26
  29.6 1.2 fusion.22
  30.9 2.5 fusion.17
  33.4 0.8 fusion.16
  34.2 26.0 %all-reduce.1 = (bf16[128,32]{0,1:T(8,128)(2,1)S(1)}, bf16[128,32]{0,1:T(8,128)(2,1)S(1)}) all-reduce(f32[128,32]{0,1:T(8,128)S(1)} %fusion.17, f32[128,32]{0,1:T(8,128)S(1)} %fusion.16), channel_id=1, replica_groups=mesh['dp'=4,'fsdp'=8] {'fsdp'}, use_global_device_ids=true, to_apply=%region_3.0 | all-reduce | flops 8192 | bytes 49152 | tf_op jit(solution)/shard_map/psum | solution.py:53
  60.2 0.7 multiply_convert_fusion.1
  60.9 2.5 copy.28
  63.4 0.8 multiply_convert_fusion
  64.2 2.5 copy.30
  66.7 0.5 all-gather.2.cloned.1.call-update
  67.3 32.9 %convolution_bitcast_fusion = f32[16384,128]{0,1:T(8,128)} fusion(bf16[16384,2048]{1,0:T(8,128)(2,1)} %param.15, bf16[128,2048]{1,0:T(8,128)(2,1)S(1)} %copy-done.2, pred[128]{0:T(512)(128)(4,1)S(1)} %iota_compare_fusion.1), kind=kOutput, calls=%fused_computation | convolution fusion | flops 8590196736 | bytes 76021888 | tf_op jit(solution)/shard_map/dot_general | solution.py:73
  100.2 0.7 copy-done.8
  100.9 0.1 copy.29
  100.9 0.1 copy.31
  101.0 67.6 %all-reduce.5.cloned.1.call-done = (bf16[2048,16,32]{0,1,2:T(8,128)(2,1)}, bf16[16,32,2048]{2,0,1:T(8,128)(2,1)}) async-done(((bf16[2048,16,32]{0,1,2:T(8,128)(2,1)}, bf16[16,32,2048]{2,0,1:T(8,128)(2,1)}), (bf16[2048,16,32]{0,1,2:T(8,128)(2,1)}, bf16[16,32,2048]{2,0,1:T(8,128)(2,1)})) %all-reduce.5.cloned.1.call-update) | async-done | bytes 4194320 | tf_op jit(solution)/shard_map/psum | solution.py:103
  168.6 3.7 %fusion.9 = (f32[8,32]{0,1:T(8,128)S(1)}, f32[8,2048]{1,0:T(8,128)S(1)}, f32[8,2048,32]{1,0,2:T(8,128)}) fusion(bf16[2048,16,32]{0,1,2:T(8,128)(2,1)} %get-tuple-element.33, s32[16]{0:T(128)S(1)} %copy-done.10, s32[8]{0:T(128)S(1)} %iota_add_fusion), kind=kOutput, calls=%fused_computation.18 | convolution fusion | flops 18857856 | bytes 4260960 | tf_op jit(solution)/shard_map/st,ftr->sfr/dot_general | solution.py:108
  172.3 0.1 fusion.38
  172.5 2.0 fusion.11
  174.5 31.0 %all-reduce = (f32[8]{0:T(128)S(1)}, f32[8,32]{0,1:T(8,128)S(1)}, f32[8,32]{0,1:T(8,128)S(1)}) all-reduce(f32[8]{0:T(128)S(1)} %get-tuple-element.37, f32[8,32]{0,1:T(8,128)S(1)} %get-tuple-element.26, f32[8,32]{0,1:T(8,128)S(1)} %get-tuple-element.25), channel_id=1, replica_groups=mesh['dp'=4,'fsdp'=8] {'fsdp'}, use_global_device_ids=true, to_apply=%region_12.13 | all-reduce | flops 520 | bytes 4160 | tf_op jit(solution)/shard_map/psum | solution.py:118
  205.5 0.7 copy.35
  206.2 1.9 rsqrt_multiply_fusion.1
  208.1 2.5 %copy.33 = f32[8,2048,32]{1,2,0:T(8,128)} copy(f32[8,2048,32]{1,0,2:T(8,128)S(1)} %rsqrt_multiply_fusion.1) | data formatting | bytes 4194304
  210.7 0.7 copy.36
  211.4 2.0 rsqrt_multiply_fusion
  213.4 2.5 %copy.34 = f32[8,32,2048]{2,1,0:T(8,128)} copy(f32[8,32,2048]{2,0,1:T(8,128)S(1)} %rsqrt_multiply_fusion) | data formatting | bytes 4194304
  215.9 23.9 %fusion.39 = f32[128,2048]{1,0:T(8,128)S(1)} fusion(bf16[128,16384]{1,0:T(8,128)(2,1)} %all-gather.2.cloned.1.call-done, bf16[16384,2048]{1,0:T(8,128)(2,1)} %param.15), kind=kOutput, calls=%fused_computation.60 | convolution fusion | flops 8589934592 | bytes 72351744 | tf_op jit(solution)/shard_map/dot_general | solution.py:39
  239.8 1.3 fusion.5
  241.1 2.3 fusion.6
  243.4 1.0 copy.32
  (37 shorter events, 0.3 us)
Async XLA Ops:
  8.0 25.4 %copy-start = (bf16[16,32,2048]{2,1,0:T(8,128)(2,1)S(1)}, bf16[16,32,2048]{2,1,0:T(8,128)(2,1)}, u32[]{:S(2)}) copy-start(bf16[16,32,2048]{2,1,0:T(8,128)(2,1)} %param.17) | copy-start | bytes 6291460
  8.0 160.6 %all-reduce.5.cloned.1.call-start = ((), (), s32[]{:S(2)}) async-start(), calls=%async_computation.3 | async-start | bytes 8388608 | tf_op jit(solution)/shard_map/psum | solution.py:103
  8.9 24.5 %copy-start.2 = (bf16[128,2048]{1,0:T(8,128)(2,1)S(1)}, bf16[128,2048]{1,0:T(8,128)(2,1)}, u32[]{:S(2)}) copy-start(bf16[128,2048]{1,0:T(8,128)(2,1)} %param.21) | copy-start | bytes 1572868
  30.8 29.3 %copy-start.1 = (bf16[128,2048]{1,0:T(8,128)(2,1)}, bf16[128,2048]{1,0:T(8,128)(2,1)S(1)}, u32[]{:S(2)}) copy-start(bf16[128,2048]{1,0:T(8,128)(2,1)S(1)} %fusion.22) | copy-start | bytes 1572868
  66.6 149.2 %all-gather.2.cloned.1.call-start = ((), (), s32[]{:S(2)}) async-start(), calls=%async_computation.1 | async-start | bytes 4718592 | tf_op jit(solution)/shard_map/all_gather | solution.py:40
  67.2 173.9 %reduce-scatter.2.cloned.1.call-start = ((), (), s32[]{:S(2)}) async-start(), calls=%async_computation.2 | async-start | bytes 9437184 | tf_op jit(solution)/shard_map/reduce_scatter | solution.py:72
  100.2 0.7 copy-start.8
  100.2 0.8 copy-start.9
  100.2 68.4 %copy-start.10 = (s32[16]{0:T(128)S(1)}, s32[16]{0:T(128)}, u32[]{:S(2)}) copy-start(s32[16]{0:T(128)} %param.19) | copy-start | bytes 196
  168.6 3.7 %copy-start.6 = (f32[8,2048]{1,0:T(8,128)S(1)}, f32[8,2048]{1,0:T(8,128)}, u32[]{:S(2)}) copy-start(f32[8,2048]{1,0:T(8,128)} %param.22) | copy-start | bytes 196612
  168.6 3.8 %copy-start.3 = (bf16[16,32,2048]{2,0,1:T(8,128)(2,1)S(1)}, bf16[16,32,2048]{2,0,1:T(8,128)(2,1)}, u32[]{:S(2)}) copy-start(bf16[16,32,2048]{2,0,1:T(8,128)(2,1)} %get-tuple-element.34) | copy-start | bytes 6291460
  172.5 33.7 %copy-start.4 = (f32[8,2048]{1,0:T(8,128)}, f32[8,2048]{1,0:T(8,128)S(1)}, u32[]{:S(2)}) copy-start(f32[8,2048]{1,0:T(8,128)S(1)} %get-tuple-element.38) | copy-start | bytes 196612
  208.1 3.2 %copy-start.7 = (f32[8,2048]{1,0:T(8,128)S(1)}, f32[8,2048]{1,0:T(8,128)}, u32[]{:S(2)}) copy-start(f32[8,2048]{1,0:T(8,128)} %param.25) | copy-start | bytes 196612
  211.4 2.0 copy-start.5
Sparse Core Ops, SparseCore 0:
  66.8 101.8 all-reduce.4
Sparse Core Ops, SparseCore 1:
  69.3 44.9 all-gather.1
  116.4 89.4 reduce-scatter.1
where the time goes:
time: 252 us
  blocking collectives  75.1 us (30%)
  matrix products  70.9 us (28%)
  waiting for transfers between devices  68.2 us (27%)
  between operations  16.3 us (6%)
  local copies, waits for them, and re-layouts  13.2 us (5%)
  other arithmetic  8.13 us (3%)
    psum x1, waiting for transfers between devices, on_device(): lax.psum(down_gradient.astype(jnp.bfloat16), 'dp').astype(jnp.float32)  67.6 us
    dot_general x1, matrix products, on_device(): lax.dot_general(weight_rows, output_gradient, contract_last, preferred_el...  32.9 us
    psum x1, blocking collectives, on_device(): lax.psum((jnp.sum(sq_a, axis=1), jnp.sum(sq_b, axis=2), jnp.sum(row_a_new...  31 us
    psum x1, blocking collectives, on_device(): inner = lax.psum(inner_part, 'fsdp')  26 us
    dot_general x1, matrix products, on_device(): jnp.dot(lax.all_gather(normalized_input, 'fsdp', axis=1, tiled=True), wei...  23.9 us
    psum x1, blocking collectives, on_device(): power = lax.psum(jnp.sum(local_f * local_f, axis=1, keepdims=True), 'fsdp')  18.1 us
    unnamed x29, local copies, waits for them, and re-layouts  8.25 us
  transfers between devices with their start and end apart: 3, of which 1 were waited for; matrix products, arithmetic and copies ran while one was open for 30% of the time, Pallas kernels for 0%

commit v1 on v0

v1 whole, which is shorter than its diff:
```python
import jax
import jax.numpy as jnp
from jax import lax
from jax.sharding import PartitionSpec as P

ADAPTER_SCALE = 0.5
BETA_TWO = 0.9
SQ_EPS = 1e-30
RMS_EPS = 1e-05

CONTRACT_LAST = (((1,), (1,)), ((), ()))


def on_device(
    inputs,
    norm_gain_vector,
    weight,
    down_adapters,
    up_adapters,
    tenant,
    tenant_slot_index,
    live_row_count,
    cotangent,
    down_row_factor,
    down_column_factor,
    up_row_factor,
    up_column_factor,
):
    rows, local = inputs.shape
    width = weight.shape[0]
    tenants, rank = down_adapters.shape[1:]
    owned = down_row_factor.shape[0]
    f32, bf16 = jnp.float32, jnp.bfloat16
    xf = inputs.astype(f32)
    gained = (xf * norm_gain_vector.astype(f32)).astype(bf16)
    live = lax.iota(jnp.int32, rows) < live_row_count[0]
    grad_out = jnp.where(live[:, None], cotangent, jnp.zeros_like(cotangent))
    gained_all = lax.all_gather(gained, "fsdp", axis=1, tiled=True)
    grad_in = lax.psum_scatter(
        lax.dot_general(weight, grad_out, CONTRACT_LAST, preferred_element_type=f32).astype(bf16),
        "fsdp",
        scatter_dimension=0,
        tiled=True,
    )
    pick = tenant[:, None] == lax.iota(jnp.int32, tenants)[None, :]
    pick_f = pick.astype(f32)
    down = down_adapters.reshape(local, tenants * rank)
    up = up_adapters.reshape(tenants * rank, local)
    inner_all = jnp.dot(gained, down, preferred_element_type=f32)
    back_all = lax.dot_general(grad_out, up, CONTRACT_LAST, preferred_element_type=f32)

    def own(z):
        return jnp.sum(z.reshape(rows, tenants, rank) * pick_f[:, :, None], axis=1)

    packed = lax.psum(
        jnp.concatenate(
            [own(inner_all), own(back_all), jnp.sum(xf * xf, axis=1, keepdims=True)], axis=1
        ),
        "fsdp",
    )
    scale = lax.rsqrt(packed[:, 2 * rank :] / width + RMS_EPS)
    inner = packed[:, :rank] * scale
    back = packed[:, rank : 2 * rank]

    def spread(z, mask):
        return (z.astype(bf16)[:, None, :] * mask.astype(bf16)[:, :, None]).reshape(z.shape[0], -1)

    adapted = jnp.dot(spread(inner, pick), up, preferred_element_type=f32)
    frozen = jnp.dot(gained_all, weight, preferred_element_type=f32)
    projected = (frozen * scale + ADAPTER_SCALE * adapted).astype(bf16)
    adapter_in = lax.dot_general(down, spread(back, pick), CONTRACT_LAST, preferred_element_type=f32)
    grad_t = (grad_in.astype(f32) + ADAPTER_SCALE * adapter_in).astype(bf16)

    slot = jnp.sum(jnp.where(pick, tenant_slot_index[None, :], 0), axis=1)
    small = jnp.concatenate([inner, back * scale, slot.astype(f32)[:, None]], axis=1)
    small_all = lax.all_gather(small, "dp", axis=0, tiled=True)
    rows_all = lax.all_gather(gained, "dp", axis=0, tiled=True)
    grad_all = lax.all_gather(grad_out, "dp", axis=0, tiled=True)
    mine = lax.iota(jnp.int32, owned) + lax.axis_index("dp") * owned
    route = small_all[:, 2 * rank :].astype(jnp.int32) == mine[None, :]
    first = (((0,), (0,)), ((), ()))
    ga = ADAPTER_SCALE * lax.dot_general(
        spread(small_all[:, rank : 2 * rank], route), rows_all, first, preferred_element_type=f32
    ).reshape(owned, rank, local)
    gb = ADAPTER_SCALE * lax.dot_general(
        spread(small_all[:, :rank], route), grad_all, first, preferred_element_type=f32
    ).reshape(owned, rank, local)
    sq_a = ga * ga + SQ_EPS
    sq_b = gb * gb + SQ_EPS
    row_a_new = BETA_TWO * down_row_factor + (1.0 - BETA_TWO) * (jnp.sum(sq_a, axis=1) / rank)
    col_b_new = BETA_TWO * up_column_factor + (1.0 - BETA_TWO) * (jnp.sum(sq_b, axis=1) / rank)
    sums = lax.psum(
        jnp.concatenate(
            [jnp.sum(sq_a, axis=2), jnp.sum(sq_b, axis=2), jnp.sum(row_a_new, axis=1)[:, None]],
            axis=1,
        ),
        "fsdp",
    )
    col_a_new = BETA_TWO * down_column_factor + (1.0 - BETA_TWO) * (sums[:, :rank] / width)
    row_b_new = BETA_TWO * up_row_factor + (1.0 - BETA_TWO) * (sums[:, rank : 2 * rank] / width)
    mean_a = sums[:, 2 * rank] / width
    mean_b = jnp.sum(row_b_new, axis=1) / rank
    update_a = ga * lax.rsqrt(row_a_new[:, None, :] * col_a_new[:, :, None] / mean_a[:, None, None])
    update_b = gb * lax.rsqrt(row_b_new[:, :, None] * col_b_new[:, None, :] / mean_b[:, None, None])
    return (
        projected,
        grad_t,
        jnp.swapaxes(update_a, 1, 2),
        update_b,
        row_a_new,
        col_a_new,
        row_b_new,
        col_b_new,
    )


def solution(mesh):
    return jax.shard_map(
        on_device,
        mesh=mesh,
        in_specs=(
            P("dp", "fsdp"),
            P("fsdp"),
            P(None, "fsdp"),
            P("fsdp", None, None),
            P(None, None, "fsdp"),
            P("dp"),
            P(),
            P("dp"),
            P("dp", "fsdp"),
            P("dp", "fsdp"),
            P("dp", None),
            P("dp", None),
            P("dp", "fsdp"),
        ),
        out_specs=(
            P("dp", "fsdp"),
            P("fsdp", "dp"),
            P("dp", "fsdp", None),
            P("dp", None, "fsdp"),
            P("dp", "fsdp"),
            P("dp", None),
            P("dp", None),
            P("dp", "fsdp"),
        ),
        check_vma=False,
    )
```

time: 252 us -> 198 us (0.79)
  waiting for transfers between devices: 68.2 us -> 45.6 us
  blocking collectives: 75.1 us -> 56.8 us
  local copies, waits for them, and re-layouts: 13.2 us -> 2.21 us
  matrix products: 70.9 us -> 67.2 us
  other arithmetic: 8.13 us -> 10.8 us
    psum x1 -> x0, waiting for transfers between devices: 67.6 us -> none  [on_device(): lax.psum(down_gradient.astype(jnp.bfloat16), 'dp').astype(jnp.float32)]
    psum x3 -> x2, blocking collectives: 75.1 us -> 46.4 us  [the longest x1 30.5 us: on_device(): lax.psum(jnp.concatenate([own(inner_all), own(back_all), jnp.sum(xf * xf,...]
    reduce_scatter x1, waiting for transfers between devices: 0.01 us -> 25 us  [on_device(): lax.psum_scatter(lax.dot_general(weight, grad_out, CONTRACT_LAST, preferr...]
    all_gather x1 -> x3, waiting for transfers between devices: 0.01 us -> 19.9 us  [the longest x1 19.9 us: on_device(): gained_all = lax.all_gather(gained, 'fsdp', axis=1, tiled=True)]
    all_gather x0 -> x1, blocking collectives: none -> 10.4 us  [on_device(): small_all = lax.all_gather(small, 'dp', axis=0, tiled=True)]
    unnamed x29 -> x31, local copies, waits for them, and re-layouts: 8.25 us -> 2.12 us
    convert_element_type x2 -> x0, local copies, waits for them, and re-layouts: 4.94 us -> none  [the longest x1 2.47 us: on_device(): down_gradient.astype(jnp.bfloat16)]
    dot_general x10 -> x8, matrix products: 70.9 us -> 67.2 us  [the longest x1 30.1 us: on_device(): lax.dot_general(weight, grad_out, CONTRACT_LAST, preferred_element_type=f32)]
  transfers between devices with their start and end apart: 3 -> 4, of which waited for: 1 -> 2; matrix products, arithmetic and copies ran while one was open for 30% -> 37% of each run, Pallas kernels for 0% -> 0%
where the time goes in v1:
time: 198 us; the launch traced here: 197 us
  matrix products  67.2 us (34%)
  blocking collectives  56.8 us (29%)
  waiting for transfers between devices  45.6 us (23%)
  between operations  14.7 us (7%)
  other arithmetic  10.8 us (5%)
  local copies, waits for them, and re-layouts  2.21 us (1%)
    psum x1, blocking collectives, on_device(): lax.psum(jnp.concatenate([own(inner_all), own(back_all), jnp.sum(xf * xf,...  30.5 us
    dot_general x1, matrix products, on_device(): lax.dot_general(weight, grad_out, CONTRACT_LAST, preferred_element_type=f32)  30.1 us
    reduce_scatter x1, waiting for transfers between devices, on_device(): lax.psum_scatter(lax.dot_general(weight, grad_out, CONTRACT_LAST, preferr...  25 us
    dot_general x1, matrix products, on_device(): frozen = jnp.dot(gained_all, weight, preferred_element_type=f32)  24.7 us
    all_gather x1, waiting for transfers between devices, on_device(): gained_all = lax.all_gather(gained, 'fsdp', axis=1, tiled=True)  19.9 us
    psum x1, blocking collectives, on_device(): lax.psum(jnp.concatenate([jnp.sum(sq_a, axis=2), jnp.sum(sq_b, axis=2), j...  15.9 us
    all_gather x1, blocking collectives, on_device(): small_all = lax.all_gather(small, 'dp', axis=0, tiled=True)  10.4 us
  transfers between devices with their start and end apart: 4, of which 2 were waited for; matrix products, arithmetic and copies ran while one was open for 37% of the time, Pallas kernels for 0%

profile of v1, /device:TPU:0, one launch (start us, length us, event | category | flops | bytes accessed | tf_op | source)
XLA Modules:
  0.0 197.5 jit_solution(12093465485129425012)
XLA Ops:
  7.2 0.8 convert_element_type.74
  8.1 2.0 %fusion.24 = (f32[128]{0:T(128)S(1)}, bf16[128,2048]{1,0:T(8,128)(2,1)}) fusion(bf16[128,2048]{1,0:T(8,128)(2,1)} %param.13, f32[2048]{0:T(1024)S(1)} %convert_element_type.74), kind=kLoop, calls=%fused_computation.33 | loop fusion | flops 1310592 | bytes 1057280 | tf_op jit(solution)/shard_map/reduce_sum | solution.py:57
  10.1 0.0 all-gather.8.cloned.1.call-start
  10.8 1.9 broadcast_select_fusion
  12.7 0.0 all-gather.4.cloned.1.call-start
  12.8 0.7 all-gather.4.cloned.1.call-update
  13.5 30.1 %fusion = bf16[16384,128]{0,1:T(8,128)(2,1)} fusion(bf16[128,2048]{1,0:T(8,128)(2,1)} %broadcast_select_fusion, bf16[16384,2048]{1,0:T(8,128)(2,1)} %param.15), kind=kOutput, calls=%fused_computation.1 | convolution fusion | flops 8592031744 | bytes 71827456 | tf_op jit(solution)/shard_map/dot_general | solution.py:40
  43.7 0.6 copy-done.13
  44.3 0.4 copy-done.1
  44.7 0.7 fusion.19
  45.4 0.1 copy-done.3
  45.5 0.7 fusion.20
  46.2 30.5 %psum.14 = f32[128,65]{0,1:T(8,128)S(1)} all-reduce(f32[128,65]{0,1:T(8,128)S(1)} %pad_maximum_fusion), channel_id=1, replica_groups=mesh['dp'=4,'fsdp'=8] {'fsdp'}, use_global_device_ids=true, to_apply=%region_3.4 | all-reduce | flops 8320 | bytes 66560 | tf_op jit(solution)/shard_map/psum | solution.py:55
  76.7 0.1 select_reduce_fusion
  76.8 10.4 %all_gather.13 = f32[512,65]{0,1:T(8,128)S(1)} all-gather(f32[128,65]{0,1:T(8,128)S(1)} %pad_maximum_fusion.1), channel_id=1, replica_groups=mesh['dp'=4,'fsdp'=8] {'dp'}, dimensions={0}, use_global_device_ids=true | all-gather | bytes 166400 | tf_op jit(solution)/shard_map/all_gather | solution.py:76
  87.3 0.1 compare_convert_fusion
  87.4 3.8 %fusion.12 = (f32[8,32]{1,0:T(8,128)S(1)}, f32[8,2048]{1,0:T(8,128)S(1)}, f32[8,32,2048]{2,1,0:T(8,128)}) fusion(bf16[512,2048]{1,0:T(8,128)(2,1)} %all-gather.6.cloned.1.call-done, bf16[512,8]{0,1:T(8,128)(2,1)S(1)} %compare_convert_fusion, bf16[512,32]{0,1:T(8,128)(2,1)S(1)} %get-tuple-element.29), kind=kOutput, calls=%fused_computation.22 | convolution fusion | flops 539606784 | bytes 4301824 | tf_op jit(solution)/shard_map/dot_general | solution.py:82
  91.2 0.1 fusion.47
  91.4 0.1 copy.21
  91.4 3.8 %fusion.14 = (f32[8,2048]{1,0:T(8,128)S(1)}, f32[8,32]{1,0:T(8,128)S(1)}, f32[8,32,2048]{2,1,0:T(8,128)}) fusion(bf16[512,2048]{1,0:T(8,128)(2,1)} %all-gather.8.cloned.1.call-done, bf16[512,32]{0,1:T(8,128)(2,1)S(1)} %get-tuple-element.28, bf16[512,8]{0,1:T(8,128)(2,1)S(1)} %compare_convert_fusion), kind=kOutput, calls=%fused_computation.24 | convolution fusion | flops 539606784 | bytes 4301824 | tf_op jit(solution)/shard_map/dot_general | solution.py:85
  95.2 0.1 pad_maximum_fusion.2
  95.3 15.9 %psum.15 = f32[8,65]{1,0:T(8,128)S(1)} all-reduce(f32[8,65]{1,0:T(8,128)S(1)} %pad_maximum_fusion.2), channel_id=1, replica_groups=mesh['dp'=4,'fsdp'=8] {'fsdp'}, use_global_device_ids=true, to_apply=%region_10.11 | all-reduce | flops 520 | bytes 4160 | tf_op jit(solution)/shard_map/psum | solution.py:92
  111.2 0.2 multiply_reduce_fusion
  111.4 0.2 fusion.46
  111.7 3.4 %bitcast_multiply_fusion = f32[8,2048,32]{1,2,0:T(8,128)} fusion(f32[8,32,2048]{2,1,0:T(8,128)} %get-tuple-element.34, f32[8]{0:T(128)S(1)} %multiply_reduce_fusion, f32[8,32]{1,0:T(8,128)S(1)} %get-tuple-element.31, f32[8,2048]{1,0:T(8,128)S(1)} %get-tuple-element.23), kind=kLoop, calls=%fused_computation.17 | loop fusion | flops 1572864 | bytes 4260896 | tf_op jit(solution)/shard_map/mul | solution.py:103
  115.1 1.8 rsqrt_multiply_fusion
  116.9 19.9 %all-gather.4.cloned.1.call-done = bf16[128,16384]{1,0:T(8,128)(2,1)} async-done(((bf16[128,2048]{1,0:T(8,128)(2,1)}), bf16[128,16384]{1,0:T(8,128)(2,1)}) %all-gather.4.cloned.1.call-update) | async-done | bytes 4194320 | tf_op jit(solution)/shard_map/all_gather | solution.py:38
  136.8 24.7 %convolution_multiply_fusion.2 = f32[128,2048]{1,0:T(8,128)S(1)} fusion(bf16[128,16384]{1,0:T(8,128)(2,1)} %all-gather.4.cloned.1.call-done, bf16[16384,2048]{1,0:T(8,128)(2,1)} %param.15, f32[128]{0:T(128)S(1)} %fusion.45), kind=kOutput, calls=%fused_computation.11 | convolution fusion | flops 8590196736 | bytes 72352256 | tf_op jit(solution)/shard_map/dot_general | solution.py:69
  161.5 1.3 fusion.6
  162.8 25.0 %reduce-scatter.2.cloned.1.call-done = bf16[2048,128]{0,1:T(8,128)(2,1)} async-done(((bf16[16384,128]{0,1:T(8,128)(2,1)}), bf16[2048,128]{0,1:T(8,128)(2,1)}) %reduce-scatter.2.cloned.1.call-update) | async-done | bytes 524304 | tf_op jit(solution)/shard_map/reduce_scatter | solution.py:39
  187.8 2.2 %fusion.7 = bf16[2048,128]{0,1:T(8,128)(2,1)S(1)} fusion(bf16[2048,16,32]{0,2,1:T(8,128)(2,1)} %param.16, bf16[2048,128]{0,1:T(8,128)(2,1)} %reduce-scatter.2.cloned.1.call-done, bf16[128,32]{0,1:T(8,128)(2,1)S(1)} %slice.58, bf16[128,16]{0,1:T(8,128)(2,1)S(1)} %get-tuple-element.32), kind=kOutput, calls=%fused_computation.13 | convolution fusion | flops 269549568 | bytes 3158016 | tf_op jit(solution)/shard_map/dot_general | solution.py:71
  189.9 1.0 copy.22
  (48 shorter events, 0.3 us)
Async XLA Ops:
  7.2 37.2 %copy-start = (bf16[16,32,2048]{2,1,0:T(8,128)(2,1)S(1)}, bf16[16,32,2048]{2,1,0:T(8,128)(2,1)}, u32[]{:S(2)}) copy-start(bf16[16,32,2048]{2,1,0:T(8,128)(2,1)} %param.17) | copy-start | bytes 6291460
  7.2 80.2 %all-gather.6.cloned.1.call-start = ((), (), s32[]{:S(2)}) async-start(), calls=%async_computation.3 | async-start | bytes 2621440 | tf_op jit(solution)/shard_map/all_gather | solution.py:77
  10.1 81.4 %all-gather.8.cloned.1.call-start = ((), (), s32[]{:S(2)}) async-start(), calls=%async_computation.4 | async-start | bytes 2621440 | tf_op jit(solution)/shard_map/all_gather | solution.py:78
  12.7 124.1 %all-gather.4.cloned.1.call-start = ((), (), s32[]{:S(2)}) async-start(), calls=%async_computation.1 | async-start | bytes 4718592 | tf_op jit(solution)/shard_map/all_gather | solution.py:38
  13.5 174.3 %reduce-scatter.2.cloned.1.call-start = ((), (), s32[]{:S(2)}) async-start(), calls=%async_computation.2 | async-start | bytes 4718592 | tf_op jit(solution)/shard_map/reduce_scatter | solution.py:39
  43.7 0.7 copy-start.13
  43.7 1.1 copy-start.1
  43.7 1.8 copy-start.2
  43.7 1.8 copy-start.3
  44.7 32.0 %copy-start.14 = (s32[16]{0:T(128)S(1)}, s32[16]{0:T(128)}, u32[]{:S(2)}) copy-start(s32[16]{0:T(128)} %param.19) | copy-start | bytes 196
  87.4 3.8 %copy-start.7 = (f32[8,2048]{1,0:T(8,128)S(1)}, f32[8,2048]{1,0:T(8,128)}, u32[]{:S(2)}) copy-start(f32[8,2048]{1,0:T(8,128)} %param.22) | copy-start | bytes 196612
  91.3 20.3 %copy-start.5 = (f32[8,2048]{1,0:T(8,128)}, f32[8,2048]{1,0:T(8,128)S(1)}, u32[]{:S(2)}) copy-start(f32[8,2048]{1,0:T(8,128)S(1)} %get-tuple-element.23) | copy-start | bytes 196612
  91.4 20.0 %copy-start.11 = (f32[8,32]{1,0:T(8,128)S(1)}, f32[8,32]{1,0:T(8,128)}, u32[]{:S(2)}) copy-start(f32[8,32]{1,0:T(8,128)} %param.24) | copy-start | bytes 3076
  91.4 20.0 %copy-start.12 = (f32[8,32]{1,0:T(8,128)S(1)}, f32[8,32]{1,0:T(8,128)}, u32[]{:S(2)}) copy-start(f32[8,32]{1,0:T(8,128)} %param.23) | copy-start | bytes 3076
  91.4 20.2 %copy-start.8 = (f32[8,2048]{1,0:T(8,128)S(1)}, f32[8,2048]{1,0:T(8,128)}, u32[]{:S(2)}) copy-start(f32[8,2048]{1,0:T(8,128)} %param.25) | copy-start | bytes 196612
  111.6 3.5 %copy-start.10 = (f32[8,32]{1,0:T(8,128)}, f32[8,32]{1,0:T(8,128)S(1)}, u32[]{:S(2)}) copy-start(f32[8,32]{1,0:T(8,128)S(1)} %get-tuple-element.31) | copy-start | bytes 3076
  111.6 3.5 %copy-start.9 = (f32[8,32]{1,0:T(8,128)}, f32[8,32]{1,0:T(8,128)S(1)}, u32[]{:S(2)}) copy-start(f32[8,32]{1,0:T(8,128)S(1)} %get-tuple-element.21) | copy-start | bytes 3076
  111.7 3.5 %copy-start.6 = (f32[8,2048]{1,0:T(8,128)}, f32[8,2048]{1,0:T(8,128)S(1)}, u32[]{:S(2)}) copy-start(f32[8,2048]{1,0:T(8,128)S(1)} %multiply_add_fusion.2) | copy-start | bytes 196612
  111.7 3.5 %copy-start.4 = (f32[8,32,2048]{2,1,0:T(8,128)S(1)}, f32[8,32,2048]{2,1,0:T(8,128)}, u32[]{:S(2)}) copy-start(f32[8,32,2048]{2,1,0:T(8,128)} %get-tuple-element.35) | copy-start | bytes 6291460
Sparse Core Ops, SparseCore 0:
  10.4 37.9 all-gather.5
  50.8 36.2 all-gather.7
  89.3 47.5 all-gather.3
  139.0 48.7 reduce-scatter.1

commit v2 on v1

v2 whole, which is shorter than its diff:
```python
import functools

import jax
import jax.numpy as jnp
from jax import lax
from jax.experimental import pallas as pl
from jax.experimental.pallas import tpu as pltpu
from jax.sharding import PartitionSpec as P

ADAPTER_SCALE = 0.5
BETA_TWO = 0.9
SQ_EPS = 1e-30
RMS_EPS = 1e-05
BUFFERS = 3
NT = (((1,), (1,)), ((), ()))
TN = (((0,), (0,)), ((), ()))
F32, BF16 = jnp.float32, jnp.bfloat16
MESH = pl.DeviceIdType.MESH


def xor(a, b, count):
    out, bit = 0, 1
    while bit < count:
        out = out + ((a // bit + b // bit) % 2) * bit
        bit *= 2
    return out


def kernel(
    ndp, n, rank, tenants, owned, width,
    gained, grad, meta, down, up, weight,
    projected, grad_t, ga, gb, sum_a, sum_b, stats,
    wbuf, ag, dpx, dpg, acc, part, psend, prx, csend, uprx, dnrx,
    pk, pkrx, sm, smrx, st, strx, spread_a, spread_b, lanes, scale_col,
    wsem, ag_s, ag_sp, ag_r, dp_s, dp_r, pp_s, pp_r, ch_s, up_r, dn_r, pk_s, pk_r, st_s, st_r,
):
    rows, local = gained.shape
    tile = wbuf.shape[1]
    tpb = local // tile
    nq = n // 2
    count = 2 * nq * tpb
    d = lax.axis_index("dp")
    f = lax.axis_index("fsdp")
    q, c = f // 2, f % 2
    mate = 2 * q + 1 - c

    def remote(src, dst, ssem, rsem, **where):
        return pltpu.make_async_remote_copy(
            src_ref=src, dst_ref=dst, send_sem=ssem, recv_sem=rsem,
            device_id=where, device_id_type=MESH,
        )

    def start_row(i):
        i2 = i % count
        back = i // count == 0
        s, r = i2 // (2 * tpb), i2 % (2 * tpb)
        half = r // tpb
        t = xor(q, jnp.where(back, nq - 1 - s, s), nq)
        core = jnp.where(back, (1 - c) * (1 - half) + c * half, c * (1 - half) + (1 - c) * half)
        return (2 * t + core) * local + (r % tpb) * tile

    def load(i):
        return pltpu.make_async_copy(
            weight.at[pl.ds(pl.multiple_of(start_row(i), tile), tile), :],
            wbuf.at[i % BUFFERS], wsem.at[i % BUFFERS],
        )

    for i in range(BUFFERS):
        load(jnp.int32(i)).start()

    barrier = pltpu.get_barrier_semaphore()
    for k in range(1, n):
        pl.semaphore_signal(barrier, inc=1, device_id={"fsdp": (f + k) % n}, device_id_type=MESH)
    for k in range(1, ndp):
        pl.semaphore_signal(barrier, inc=1, device_id={"dp": (d + k) % ndp}, device_id_type=MESH)
    pl.semaphore_wait(barrier, n - 1 + ndp - 1)

    def ag_up(slot, src):
        return remote(src, ag.at[slot], ag_s.at[slot, 0], ag_r.at[slot], fsdp=(f + 2) % n)

    def ag_down(slot, src):
        return remote(src, ag.at[slot], ag_s.at[slot, 1], ag_r.at[slot], fsdp=(f + n - 2) % n)

    def ag_mate(slot, src):
        return remote(src, ag.at[slot], ag_sp.at[slot], ag_r.at[slot], fsdp=mate)

    @pl.when(q + 1 < nq)
    def _():
        ag_up(f, gained).start()

    @pl.when(q > 0)
    def _():
        ag_down(f, gained).start()

    ag_mate(f, gained).start()

    def dp_copy(which, src, dst, k):
        return remote(src, dst.at[d], dp_s.at[which, k], dp_r.at[which, k], dp=(d + k) % ndp)

    for k in range(1, ndp):
        dp_copy(0, gained, dpx, k).start()
        dp_copy(1, grad, dpg, k).start()

    def ag_event(k):
        below, above = 2 * (q - k) + c, 2 * (q + k) + c

        @pl.when(q - k >= 0)
        def _():
            ag_up(below, ag.at[below]).wait_recv()

            @pl.when(q + 1 < nq)
            def _():
                ag_up(below, ag.at[below]).start()

            ag_mate(below, ag.at[below]).start()

        @pl.when(q + k < nq)
        def _():
            ag_down(above, ag.at[above]).wait_recv()

            @pl.when(q > 0)
            def _():
                ag_down(above, ag.at[above]).start()

            ag_mate(above, ag.at[above]).start()

    tenant = meta[0:1, :]
    owner = lax.broadcasted_iota(jnp.int32, (tenants * rank, rows), 0) // rank
    picked = owner.astype(F32) == tenant
    for at, lhs, rhs in ((0, down, gained), (rank, up, grad)):
        full = lax.dot_general(lhs[...], rhs[...], NT, preferred_element_type=F32)
        full = jnp.where(picked, full, 0.0).reshape(tenants, rank, rows)
        pk[at : at + rank, :] = jnp.sum(full, axis=0)
    pk[2 * rank : 2 * rank + 8, :] = meta[8:16, :]

    def pk_copy(k):
        return remote(pk, pkrx.at[k], pk_s.at[k], pk_r.at[k], fsdp=(f + k) % n)

    for k in range(1, n):
        pk_copy(k).start()
    ag[f] = gained[...]
    dpx[d] = gained[...]
    dpg[d] = grad[...]

    def chain_copy(t, rsem, rx, to):
        return remote(csend.at[t], rx.at[t], ch_s.at[t], rsem.at[t], fsdp=to)

    def chain_up(t):
        return chain_copy(t, up_r, uprx, (f + 2) % n)

    def chain_down(t):
        return chain_copy(t, dn_r, dnrx, (f + n - 2) % n)

    def mate_copy(t):
        return remote(psend.at[t], prx.at[t], pp_s.at[t], pp_r.at[t], fsdp=mate)

    def head(t):
        return ((t > q) & (q == 0)) | ((t < q) & (q == nq - 1))

    def chain(t):
        mate_copy(t).wait_recv()
        part[t] = (part[t].astype(F32) + prx[t].astype(F32)).astype(BF16)

        @pl.when((t > q) & (q > 0))
        def _():
            chain_up(t).wait_recv()
            csend[t] = (part[t].astype(F32) + uprx[t].astype(F32)).astype(BF16)

        @pl.when((t < q) & (q < nq - 1))
        def _():
            chain_down(t).wait_recv()
            csend[t] = (part[t].astype(F32) + dnrx[t].astype(F32)).astype(BF16)

        @pl.when(head(t))
        def _():
            csend[t] = part[t]

        @pl.when(t > q)
        def _():
            chain_up(t).start()

        @pl.when(t < q)
        def _():
            chain_down(t).start()

    def order(s):
        return xor(q, nq - 1 - s, nq)

    lag = min(2, nq - 1)
    period = -(-count // max(nq - 1, 1))
    in_back = min(count // period, nq - 1)

    @pl.loop(0, count)
    def _(i):
        load(i).wait()
        s, r = i // (2 * tpb), i % (2 * tpb)
        half, where = r // tpb, pl.ds(pl.multiple_of((r % tpb) * tile, tile), tile)
        t = order(s)
        out = lax.dot_general(
            wbuf[i % BUFFERS], grad[...], NT, preferred_element_type=F32
        ).astype(BF16)
        load(i + BUFFERS).start()

        @pl.when(half == 0)
        def _():
            psend[t, where, :] = out

        @pl.when(half == 1)
        def _():
            part[t, where, :] = out

        @pl.when(r == tpb - 1)
        def _():
            mate_copy(t).start()

        @pl.when((r == 2 * tpb - 1) & head(t))
        def _():
            chain(t)

        late = order(jnp.maximum(s - lag, 0))

        @pl.when((r == 2 * tpb - 1) & (s >= lag) & jnp.logical_not(head(late)))
        def _():
            chain(late)

        k = (i + 1) // period

        @pl.when(((i + 1) % period == 0) & (k < nq))
        def _():
            ag_event(k)

    total = pk[...]
    for k in range(1, n):
        pk_copy(k).wait_recv()
        total = total + pkrx[k]
    scale = lax.rsqrt(total[2 * rank : 2 * rank + 1, :] / width + RMS_EPS)
    inner = total[:rank, :] * scale
    back = total[rank : 2 * rank, :]
    sm[0:rank, :] = inner
    sm[rank : 2 * rank, :] = back * scale
    sm[2 * rank :, :] = jnp.concatenate([meta[1:2, :], total[2 * rank + 1 :, :]], axis=0)

    def sm_copy(k):
        return remote(sm, smrx.at[d], dp_s.at[2, k], dp_r.at[2, k], dp=(d + k) % ndp)

    for k in range(1, ndp):
        sm_copy(k).start()
    smrx[d] = sm[...]
    spread_a[...] = jnp.where(picked, jnp.tile(inner, (tenants, 1)), 0.0).astype(BF16)
    spread_b[...] = jnp.where(picked, jnp.tile(back, (tenants, 1)), 0.0).astype(BF16)
    scale_col[...] = jnp.broadcast_to(scale, (rows, rows)).T
    acc[...] = jnp.zeros_like(acc)

    @pl.loop(0, count)
    def _(i):
        s, r = i // (2 * tpb), i % (2 * tpb)
        half = r // tpb
        t = xor(q, s, nq)
        core = c * (1 - half) + (1 - c) * half
        slot = 2 * t + core

        @pl.when((r == 0) & (s + 1 < nq) & (s + 1 > in_back))
        def _():
            ag_event(s + 1)

        @pl.when(r == tpb)
        def _():
            ag_mate(slot, ag.at[slot]).wait_recv()

        load(count + i).wait()
        cols = pl.ds(pl.multiple_of((r % tpb) * tile, tile), tile)
        acc[...] += jnp.dot(
            ag[slot, :, cols], wbuf[(count + i) % BUFFERS], preferred_element_type=F32
        )

        @pl.when(i + BUFFERS < count)
        def _():
            load(count + i + BUFFERS).start()

        first = max(nq - lag, 0)
        for e in range(first, nq - 1):
            late = order(jnp.int32(e))

            @pl.when((i == (e - first + 1) * count // (nq - first) - 1) & jnp.logical_not(head(late)))
            def _():
                chain(late)

    for k in range(1, ndp):
        dp_copy(0, gained, dpx, k).wait_recv()
        dp_copy(1, grad, dpg, k).wait_recv()
        sm_copy(k).wait_recv()
    place = lax.broadcasted_iota(jnp.int32, (owned * rank, rows), 0) // rank + d * owned
    place = place.astype(F32)
    for at, src, dst, summed, base in ((rank, dpx, ga, sum_a, 0), (0, dpg, gb, sum_b, owned * rank)):
        lhs = jnp.concatenate(
            [
                jnp.where(
                    place == smrx[g, 2 * rank : 2 * rank + 1, :],
                    jnp.tile(smrx[g, at : at + rank, :], (owned, 1)),
                    0.0,
                ).astype(BF16)
                for g in range(ndp)
            ],
            axis=1,
        )
        step = min(512, local)
        for lo in range(0, local, step):
            rhs = src[:, :, lo : lo + step].reshape(ndp * rows, step)
            full = ADAPTER_SCALE * jnp.dot(lhs, rhs, preferred_element_type=F32)
            full = full.reshape(owned, rank, step)
            dst[:, :, lo : lo + step] = full
            sq = full * full + SQ_EPS
            summed[:, lo : lo + step] = jnp.sum(sq, axis=1)
            flat = sq.reshape(owned * rank, step)
            total = flat[:, 0:128]
            for w in range(128, step, 128):
                total = total + flat[:, w : w + 128]
            here = slice(base, base + owned * rank)
            if lo == 0:
                lanes[here, :] = total
            else:
                lanes[here, :] += total
    turned = lanes[...].T
    st[...] = jnp.sum(turned.reshape(16, 8, 2 * owned * rank), axis=0)

    def st_copy(k):
        return remote(st, strx.at[k], st_s.at[k], st_r.at[k], fsdp=(f + k) % n)

    for k in range(1, n):
        st_copy(k).start()

    chunk = min(512, local)
    for lo in range(0, local, chunk):
        cols = slice(lo, lo + chunk)
        adapted = lax.dot_general(spread_a[...], up[:, cols], TN, preferred_element_type=F32)
        wide = jnp.concatenate([scale_col[...]] * (chunk // rows), axis=1)
        projected[:, cols] = (acc[:, cols] * wide + ADAPTER_SCALE * adapted).astype(BF16)
    mate_copy(q).wait_recv()

    @pl.when(q > 0)
    def _():
        chain_up(q).wait_recv()

    @pl.when(q < nq - 1)
    def _():
        chain_down(q).wait_recv()

    for lo in range(0, local, chunk):
        here = slice(lo, lo + chunk)
        out = lax.dot_general(down[:, here], spread_b[...], TN, preferred_element_type=F32)
        out = ADAPTER_SCALE * out + part[q, here, :].astype(F32) + prx[q, here, :].astype(F32)
        lanes_up = jnp.where(q > 0, uprx[q, here, :].astype(F32), 0.0)
        lanes_dn = jnp.where(q < nq - 1, dnrx[q, here, :].astype(F32), 0.0)
        grad_t[here, :] = (out + lanes_up + lanes_dn).astype(BF16)

    whole = st[...]
    for k in range(1, n):
        st_copy(k).wait_recv()
        whole = whole + strx[k]
    stats[:, : 2 * owned * rank] = whole
    stats[:, 2 * owned * rank :] = sm[2 * rank :, :]

    for k in range(1, n):
        pk_copy(k).wait_send()
        st_copy(k).wait_send()
    for k in range(1, ndp):
        dp_copy(0, gained, dpx, k).wait_send()
        dp_copy(1, grad, dpg, k).wait_send()
        sm_copy(k).wait_send()

    @pl.loop(0, nq)
    def _(t):
        mate_copy(t).wait_send()
        slot = 2 * t + c

        @pl.when(t != q)
        def _():
            chain_up(t).wait_send()

        ag_mate(slot, ag.at[slot]).wait_send()

        @pl.when((t <= q) & (q + 1 < nq))
        def _():
            ag_up(slot, ag.at[slot]).wait_send()

        @pl.when((t >= q) & (q > 0))
        def _():
            ag_down(slot, ag.at[slot]).wait_send()


def on_device(
    ndp,
    n,
    inputs,
    norm_gain_vector,
    weight,
    down_adapters,
    up_adapters,
    tenant,
    tenant_slot_index,
    live_row_count,
    cotangent,
    down_row_factor,
    down_column_factor,
    up_row_factor,
    up_column_factor,
):
    rows, local = inputs.shape
    width = weight.shape[0]
    tenants, rank = down_adapters.shape[1:]
    owned = down_row_factor.shape[0]
    xf = inputs.astype(F32)
    gained = (xf * norm_gain_vector.astype(F32)).astype(BF16)
    live = lax.iota(jnp.int32, rows) < live_row_count[0]
    grad = jnp.where(live[:, None], cotangent, jnp.zeros_like(cotangent))
    pick = tenant[None, :] == lax.iota(jnp.int32, tenants)[:, None]
    slot = jnp.sum(jnp.where(pick, tenant_slot_index[:, None], 0), axis=0).astype(F32)
    power = jnp.sum(xf * xf, axis=1)
    factor_sum = jnp.pad(jnp.sum(down_row_factor, axis=1), (0, rows - owned))
    zero = jnp.zeros((6, rows), F32)
    meta = jnp.concatenate(
        [tenant.astype(F32)[None], slot[None], zero, power[None], factor_sum[None], zero], axis=0
    )
    down = jnp.transpose(down_adapters, (1, 2, 0)).reshape(tenants * rank, local)
    up = up_adapters.reshape(tenants * rank, local)
    tile = min(1024, local)
    nq = n // 2
    pieces = 2 * rank + 8
    cols = 2 * owned * rank
    vmem = pl.BlockSpec(memory_space=pltpu.VMEM)
    dma = pltpu.SemaphoreType.DMA
    half = pltpu.VMEM((nq, local, rows), BF16)
    projected, grad_t, ga, gb, sum_a, sum_b, stats = pl.pallas_call(
        functools.partial(kernel, ndp, n, rank, tenants, owned, width),
        out_shape=(
            jax.ShapeDtypeStruct((rows, local), BF16),
            jax.ShapeDtypeStruct((local, rows), BF16),
            jax.ShapeDtypeStruct((owned, rank, local), F32),
            jax.ShapeDtypeStruct((owned, rank, local), F32),
            jax.ShapeDtypeStruct((owned, local), F32),
            jax.ShapeDtypeStruct((owned, local), F32),
            jax.ShapeDtypeStruct((8, cols + rows), F32),
        ),
        in_specs=[vmem] * 5 + [pl.BlockSpec(memory_space=pl.ANY)],
        out_specs=(vmem,) * 7,
        scratch_shapes=[
            pltpu.VMEM((BUFFERS, tile, local), BF16),
            pltpu.VMEM((n, rows, local), BF16),
            pltpu.VMEM((ndp, rows, local), BF16),
            pltpu.VMEM((ndp, rows, local), BF16),
            pltpu.VMEM((rows, local), F32),
            half, half, half, half, half, half,
            pltpu.VMEM((pieces, rows), F32),
            pltpu.VMEM((n, pieces, rows), F32),
            pltpu.VMEM((pieces, rows), F32),
            pltpu.VMEM((ndp, pieces, rows), F32),
            pltpu.VMEM((8, cols), F32),
            pltpu.VMEM((n, 8, cols), F32),
            pltpu.VMEM((tenants * rank, rows), BF16),
            pltpu.VMEM((tenants * rank, rows), BF16),
            pltpu.VMEM((cols, 128), F32),
            pltpu.VMEM((rows, rows), F32),
            dma((BUFFERS,)),
            dma((n, 2)),
            dma((n,)),
            dma((n,)),
            dma((3, ndp)),
            dma((3, ndp)),
            dma((nq,)),
            dma((nq,)),
            dma((nq,)),
            dma((nq,)),
            dma((nq,)),
            dma((n,)),
            dma((n,)),
            dma((n,)),
            dma((n,)),
        ],
        compiler_params=pltpu.CompilerParams(
            collective_id=0, has_side_effects=True, vmem_limit_bytes=60 * 1024 * 1024
        ),
    )(gained, grad, meta, down, up, weight)

    row_a_new = BETA_TWO * down_row_factor + (1.0 - BETA_TWO) * (sum_a / rank)
    col_b_new = BETA_TWO * up_column_factor + (1.0 - BETA_TWO) * (sum_b / rank)
    sums = jnp.sum(stats[:, :cols], axis=0).reshape(2, owned, rank)
    col_a_new = BETA_TWO * down_column_factor + (1.0 - BETA_TWO) * (sums[0] / width)
    row_b_new = BETA_TWO * up_row_factor + (1.0 - BETA_TWO) * (sums[1] / width)
    kept = stats[1, cols : cols + owned]
    mean_a = (BETA_TWO * kept + (1.0 - BETA_TWO) * (jnp.sum(sums[0], axis=1) / rank)) / width
    mean_b = jnp.sum(row_b_new, axis=1) / rank
    update_a = ga * lax.rsqrt(row_a_new[:, None, :] * col_a_new[:, :, None] / mean_a[:, None, None])
    update_b = gb * lax.rsqrt(row_b_new[:, :, None] * col_b_new[:, None, :] / mean_b[:, None, None])
    return (
        projected,
        grad_t,
        jnp.swapaxes(update_a, 1, 2),
        update_b,
        row_a_new,
        col_a_new,
        row_b_new,
        col_b_new,
    )


def solution(mesh):
    return jax.shard_map(
        functools.partial(on_device, mesh.shape["dp"], mesh.shape["fsdp"]),
        mesh=mesh,
        in_specs=(
            P("dp", "fsdp"),
            P("fsdp"),
            P(None, "fsdp"),
            P("fsdp", None, None),
            P(None, None, "fsdp"),
            P("dp"),
            P(),
            P("dp"),
            P("dp", "fsdp"),
            P("dp", "fsdp"),
            P("dp", None),
            P("dp", None),
            P("dp", "fsdp"),
        ),
        out_specs=(
            P("dp", "fsdp"),
            P("fsdp", "dp"),
            P("dp", "fsdp", None),
            P("dp", None, "fsdp"),
            P("dp", "fsdp"),
            P("dp", None),
            P("dp", None),
            P("dp", "fsdp"),
        ),
        check_vma=False,
    )
```

time: 198 us -> 109 us (0.55)
  Pallas kernels: 0 us -> 89.5 us
  matrix products: 67.2 us -> 0 us
  blocking collectives: 56.8 us -> 0 us
  waiting for transfers between devices: 45.6 us -> 0 us
  between operations: 14.7 us -> 1.4 us
  other arithmetic: 10.8 us -> 14.6 us
    pallas_call x0 -> x1, Pallas kernels: none -> 89.5 us  [on_device(): pl.pallas_call(functools.partial(kernel, ndp, n, rank, tenants, owned, wi...]
    dot_general x8 -> x0, matrix products: 67.2 us -> none  [the longest x1 30.1 us: on_device(): lax.dot_general(weight, grad_out, CONTRACT_LAST, preferred_element_type=f32)]
    psum x2 -> x0, blocking collectives: 46.4 us -> none  [the longest x1 30.5 us: on_device(): lax.psum(jnp.concatenate([own(inner_all), own(back_all), jnp.sum(xf * xf,...]
    reduce_scatter x1 -> x0, waiting for transfers between devices: 25 us -> none  [on_device(): lax.psum_scatter(lax.dot_general(weight, grad_out, CONTRACT_LAST, preferr...]
    all_gather x3 -> x0, waiting for transfers between devices: 19.9 us -> none  [the longest x1 19.9 us: on_device(): gained_all = lax.all_gather(gained, 'fsdp', axis=1, tiled=True)]
    all_gather x1 -> x0, blocking collectives: 10.4 us -> none  [on_device(): small_all = lax.all_gather(small, 'dp', axis=0, tiled=True)]
    transpose x0 -> x1, other arithmetic: none -> 3.48 us  [on_device(): jnp.swapaxes(update_a, 1, 2)]
    mul x2 -> x1, other arithmetic: 3.44 us -> 0.01 us  [on_device(): row_b_new = BETA_TWO * up_row_factor + (1.0 - BETA_TWO) * (sums[1] / width)]
  transfers between devices with their start and end apart: 4 -> 0, of which waited for: 2 -> 0; matrix products, arithmetic and copies ran while one was open for 37% -> 0% of each run, Pallas kernels for 0% -> 0%
where the time goes in v2:
time: 109 us
  Pallas kernels  89.5 us (82%)
  other arithmetic  14.6 us (13%)
  local copies, waits for them, and re-layouts  3.01 us (3%)
  between operations  1.4 us (1%)
    pallas_call x1, Pallas kernels, on_device(): pl.pallas_call(functools.partial(kernel, ndp, n, rank, tenants, owned, wi...  89.5 us
    transpose x1, other arithmetic, on_device(): jnp.swapaxes(update_a, 1, 2)  3.48 us

profile of v2, /device:TPU:0, one launch (start us, length us, event | category | flops | bytes accessed | tf_op | source)
XLA Modules:
  0.0 108.5 jit_solution(10787127598324089522)
XLA Ops:
  1.3 0.8 select_reduce_fusion
  2.1 0.7 convert_bitcast_fusion.1
  2.7 1.0 reduce_sum.56
  3.7 0.7 convert_element_type.28
  4.4 2.0 %fusion.1 = (f32[128]{0:T(128)S(1)}, bf16[128,2048]{1,0:T(8,128)(2,1)}) fusion(bf16[128,2048]{1,0:T(8,128)(2,1)} %param.13, f32[2048]{0:T(1024)S(1)} %convert_element_type.28), kind=kLoop, calls=%fused_computation.5 | loop fusion | flops 1310592 | bytes 1057280 | tf_op jit(solution)/shard_map/reduce_sum | solution.py:418
  6.4 1.2 %concatenate.3.meta = f32[16,128]{1,0:T(8,128)} concatenate(f32[1,128]{1,0:T(1,128)S(1)} %convert_bitcast_fusion.1, f32[1,128]{1,0:T(1,128)S(1)} %convert_bitcast_fusion, f32[6,128]{1,0:T(8,128)S(1)} %broadcast_in_dim.52, f32[1,128]{1,0:T(1,128)S(1)} %bitcast.21, f32[1,128]{1,0:T(1,128)S(1)} %pad_bitcast_fusion, f32[6,128]{1,0:T(8,128)S(1)} %broadcast_in_dim.52), dimensions={0} | concatenate | bytes 16384 | tf_op jit(solution)/shard_map/concatenate | solution.py:421
  7.6 1.9 %broadcast_select_fusion.grad = bf16[128,2048]{1,0:T(8,128)(2,1)} fusion(bf16[128,2048]{1,0:T(8,128)(2,1)} %param.21, pred[128]{0:T(512)(128)(4,1)S(1)} %iota_compare_fusion.1), kind=kLoop, calls=%fused_computation.6 | loop fusion | flops 262144 | bytes 1048704 | tf_op jit(solution)/shard_map/jit(_where)/select_n | solution.py:415
  9.5 89.5 %shard_map.188 = (bf16[128,2048]{1,0:T(8,128)(2,1)}, bf16[2048,128]{1,0:T(8,128)(2,1)}, f32[8,32,2048]{2,1,0:T(8,128)}, f32[8,32,2048]{2,1,0:T(8,128)}, f32[8,20...) custom-call(bf16[128,2048]{1,0:T(8,128)(2,1)} %get-tuple-element.25.gained, ...), custom_call_target="tpu_custom_call" | custom-call | tf_op jit(solution)/shard_map/pallas_call | solution.py:433
  99.0 0.7 slice_reduce_fusion
  99.8 0.1 mul.115
  99.9 0.1 squeeze.10
  99.9 0.0 copy-done.9
  99.9 0.0 copy-done.10
  99.9 0.1 multiply_add_fusion.3
  100.1 0.0 copy-start.7
  100.1 0.0 copy-start.8
  100.1 0.7 fusion.2
  100.8 0.0 copy-done.3
  100.8 0.0 copy-done.6
  100.8 0.9 multiply_add_fusion
  101.7 0.0 copy-start.5
  101.7 0.0 copy-start.4
  101.7 0.0 copy-start
  101.8 3.5 %multiply_bitcast_fusion = f32[8,2048,32]{1,2,0:T(8,128)} fusion(f32[8,32,2048]{2,1,0:T(8,128)} %get-tuple-element.17, f32[8]{0:T(128)S(1)} %fusion.2, f32[8,32]{1,0:T(8,128)S(1)} %get-tuple-element.47, f32[8,2048]{1,0:T(8,128)S(1)} %get-tuple-element.46), kind=kLoop, calls=%fused_computation.1 | loop fusion | flops 1572864 | bytes 4260896 | tf_op jit(solution)/shard_map/transpose | solution.py:497
  105.2 0.0 copy-done.7
  105.2 0.0 copy-done.5
  105.2 0.0 copy-done.8
  105.2 0.0 copy-done.4
  105.3 1.7 %rsqrt_multiply_fusion = f32[8,32,2048]{2,1,0:T(8,128)} fusion(f32[8,32,2048]{2,1,0:T(8,128)S(1)} %copy-done, f32[8]{0:T(128)S(1)} %broadcast_multiply_fusion, f32[8,2048]{1,0:T(8,128)S(1)} %get-tuple-element.49, f32[8,32]{1,0:T(8,128)S(1)} %get-tuple-element.48), kind=kLoop, calls=%fused_computation | loop fusion | flops 1572864 | bytes 4260896 | tf_op jit(solution)/shard_map/mul | solution.py:493
  107.0 0.0 copy-done.2
  107.0 0.8 copy.24
  107.8 0.8 copy.25
  (14 shorter events, 0.0 us)
Async XLA Ops:
  9.5 90.4 %copy-start.9 = (f32[8,32]{1,0:T(8,128)S(1)}, f32[8,32]{1,0:T(8,128)}, u32[]{:S(2)}) copy-start(f32[8,32]{1,0:T(8,128)} %param.23) | copy-start | bytes 3076
  9.5 90.4 %copy-start.10 = (f32[8,32]{1,0:T(8,128)S(1)}, f32[8,32]{1,0:T(8,128)}, u32[]{:S(2)}) copy-start(f32[8,32]{1,0:T(8,128)} %param.24) | copy-start | bytes 3076
  9.5 91.3 %copy-start.3 = (f32[8,2048]{1,0:T(8,128)S(1)}, f32[8,2048]{1,0:T(8,128)}, u32[]{:S(2)}) copy-start(f32[8,2048]{1,0:T(8,128)} %param.22) | copy-start | bytes 196612
  9.5 91.3 %copy-start.6 = (f32[8,2048]{1,0:T(8,128)S(1)}, f32[8,2048]{1,0:T(8,128)}, u32[]{:S(2)}) copy-start(f32[8,2048]{1,0:T(8,128)} %param.25) | copy-start | bytes 196612
  100.1 5.1 %copy-start.7 = (f32[8,32]{1,0:T(8,128)}, f32[8,32]{1,0:T(8,128)S(1)}, u32[]{:S(2)}) copy-start(f32[8,32]{1,0:T(8,128)S(1)} %get-tuple-element.47) | copy-start | bytes 3076
  100.1 5.1 %copy-start.8 = (f32[8,32]{1,0:T(8,128)}, f32[8,32]{1,0:T(8,128)S(1)}, u32[]{:S(2)}) copy-start(f32[8,32]{1,0:T(8,128)S(1)} %get-tuple-element.48) | copy-start | bytes 3076
  101.7 3.5 %copy-start.5 = (f32[8,2048]{1,0:T(8,128)}, f32[8,2048]{1,0:T(8,128)S(1)}, u32[]{:S(2)}) copy-start(f32[8,2048]{1,0:T(8,128)S(1)} %get-tuple-element.46) | copy-start | bytes 196612
  101.7 3.5 %copy-start.4 = (f32[8,2048]{1,0:T(8,128)}, f32[8,2048]{1,0:T(8,128)S(1)}, u32[]{:S(2)}) copy-start(f32[8,2048]{1,0:T(8,128)S(1)} %get-tuple-element.49) | copy-start | bytes 196612
  101.7 3.5 %copy-start = (f32[8,32,2048]{2,1,0:T(8,128)S(1)}, f32[8,32,2048]{2,1,0:T(8,128)}, u32[]{:S(2)}) copy-start(f32[8,32,2048]{2,1,0:T(8,128)} %get-tuple-element.20) | copy-start | bytes 6291460
  105.3 1.7 %copy-start.2 = (bf16[128,2048]{1,0:T(8,128)(2,1)S(1)}, bf16[128,2048]{1,0:T(8,128)(2,1)}, u32[]{:S(2)}) copy-start(bf16[128,2048]{1,0:T(8,128)(2,1)} %get-tuple-element.42) | copy-start | bytes 1572868
  105.3 2.5 %copy-start.1 = (bf16[2048,128]{1,0:T(8,128)(2,1)S(1)}, bf16[2048,128]{1,0:T(8,128)(2,1)}, u32[]{:S(2)}) copy-start(bf16[2048,128]{1,0:T(8,128)(2,1)} %get-tuple-element.43) | copy-start | bytes 1572868

commit v3 on v2

--- a/solution.py
+++ b/solution.py
@@ -50,12 +50,18 @@
             device_id=where, device_id_type=MESH,
         )
 
+    def order(s):
+        low = q < nq // 2
+        at = jnp.where(low, q, nq - 1 - q)
+        t = jnp.where(s < nq - 1 - at, nq - 1 - s, s - (nq - 1 - at))
+        return jnp.where(low, t, nq - 1 - t)
+
     def start_row(i):
         i2 = i % count
         back = i // count == 0
         s, r = i2 // (2 * tpb), i2 % (2 * tpb)
         half = r // tpb
-        t = xor(q, jnp.where(back, nq - 1 - s, s), nq)
+        t = jnp.where(back, order(s), xor(q, s, nq))
         core = jnp.where(back, (1 - c) * (1 - half) + c * half, c * (1 - half) + (1 - c) * half)
         return (2 * t + core) * local + (r % tpb) * tile
 
@@ -183,12 +189,9 @@
         def _():
             chain_down(t).start()
 
-    def order(s):
-        return xor(q, nq - 1 - s, nq)
-
     lag = min(2, nq - 1)
-    period = -(-count // max(nq - 1, 1))
-    in_back = min(count // period, nq - 1)
+    period = max(count // max(nq - 1, 1), 1)
+    in_back = max(min(count // period, nq - 2), 0)
 
     @pl.loop(0, count)
     def _(i):
@@ -225,7 +228,7 @@
 
         k = (i + 1) // period
 
-        @pl.when(((i + 1) % period == 0) & (k < nq))
+        @pl.when(((i + 1) % period == 0) & (k <= in_back))
         def _():
             ag_event(k)
 
@@ -281,7 +284,7 @@
         for e in range(first, nq - 1):
             late = order(jnp.int32(e))
 
-            @pl.when((i == (e - first + 1) * count // (nq - first) - 1) & jnp.logical_not(head(late)))
+            @pl.when((i == 2 * (e - first + 1)) & jnp.logical_not(head(late)))
             def _():
                 chain(late)
 

time: 109 us -> 97.5 us (0.89)
  Pallas kernels: 89.5 us -> 77.9 us
    pallas_call x1, Pallas kernels: 89.5 us -> 77.9 us  [on_device(): pl.pallas_call(functools.partial(kernel, ndp, n, rank, tenants, owned, wi...]
where the time goes in v3:
time: 97.5 us; the launch traced here: 97 us
  Pallas kernels  77.9 us (80%)
  other arithmetic  14.6 us (15%)
  local copies, waits for them, and re-layouts  3.01 us (3%)
  between operations  1.4 us (1%)
    pallas_call x1, Pallas kernels, on_device(): pl.pallas_call(functools.partial(kernel, ndp, n, rank, tenants, owned, wi...  77.9 us
    transpose x1, other arithmetic, on_device(): jnp.swapaxes(update_a, 1, 2)  3.48 us
    reduce_sum x1, other arithmetic, on_device(): power = jnp.sum(xf * xf, axis=1)  1.99 us

profile of v3, /device:TPU:0, one launch (start us, length us, event | category | flops | bytes accessed | tf_op | source)
XLA Modules:
  0.0 97.0 jit_solution(4158522523856411517)
XLA Ops:
  1.3 0.8 select_reduce_fusion
  2.1 0.7 convert_bitcast_fusion.1
  2.7 1.0 reduce_sum.56
  3.7 0.7 convert_element_type.28
  4.4 2.0 %fusion.1 = (f32[128]{0:T(128)S(1)}, bf16[128,2048]{1,0:T(8,128)(2,1)}) fusion(bf16[128,2048]{1,0:T(8,128)(2,1)} %param.13, f32[2048]{0:T(1024)S(1)} %convert_element_type.28), kind=kLoop, calls=%fused_computation.5 | loop fusion | flops 1310592 | bytes 1057280 | tf_op jit(solution)/shard_map/reduce_sum | solution.py:421
  6.4 1.2 %concatenate.3.meta = f32[16,128]{1,0:T(8,128)} concatenate(f32[1,128]{1,0:T(1,128)S(1)} %convert_bitcast_fusion.1, f32[1,128]{1,0:T(1,128)S(1)} %convert_bitcast_fusion, f32[6,128]{1,0:T(8,128)S(1)} %broadcast_in_dim.52, f32[1,128]{1,0:T(1,128)S(1)} %bitcast.21, f32[1,128]{1,0:T(1,128)S(1)} %pad_bitcast_fusion, f32[6,128]{1,0:T(8,128)S(1)} %broadcast_in_dim.52), dimensions={0} | concatenate | bytes 16384 | tf_op jit(solution)/shard_map/concatenate | solution.py:424
  7.6 1.9 %broadcast_select_fusion.grad = bf16[128,2048]{1,0:T(8,128)(2,1)} fusion(bf16[128,2048]{1,0:T(8,128)(2,1)} %param.21, pred[128]{0:T(512)(128)(4,1)S(1)} %iota_compare_fusion.1), kind=kLoop, calls=%fused_computation.6 | loop fusion | flops 262144 | bytes 1048704 | tf_op jit(solution)/shard_map/jit(_where)/select_n | solution.py:418
  9.5 77.9 %shard_map.188 = (bf16[128,2048]{1,0:T(8,128)(2,1)}, bf16[2048,128]{1,0:T(8,128)(2,1)}, f32[8,32,2048]{2,1,0:T(8,128)}, f32[8,32,2048]{2,1,0:T(8,128)}, f32[8,20...) custom-call(bf16[128,2048]{1,0:T(8,128)(2,1)} %get-tuple-element.25.gained, ...), custom_call_target="tpu_custom_call" | custom-call | tf_op jit(solution)/shard_map/pallas_call | solution.py:436
  87.5 0.7 slice_reduce_fusion
  88.2 0.1 mul.115
  88.3 0.1 squeeze.10
  88.4 0.0 copy-done.9
  88.4 0.0 copy-done.10
  88.4 0.1 multiply_add_fusion.3
  88.5 0.0 copy-start.7
  88.5 0.0 copy-start.8
  88.6 0.7 fusion.2
  89.2 0.0 copy-done.3
  89.3 0.0 copy-done.6
  89.3 0.9 multiply_add_fusion
  90.2 0.0 copy-start.5
  90.2 0.0 copy-start.4
  90.2 0.0 copy-start
  90.2 3.5 %multiply_bitcast_fusion = f32[8,2048,32]{1,2,0:T(8,128)} fusion(f32[8,32,2048]{2,1,0:T(8,128)} %get-tuple-element.17, f32[8]{0:T(128)S(1)} %fusion.2, f32[8,32]{1,0:T(8,128)S(1)} %get-tuple-element.47, f32[8,2048]{1,0:T(8,128)S(1)} %get-tuple-element.46), kind=kLoop, calls=%fused_computation.1 | loop fusion | flops 1572864 | bytes 4260896 | tf_op jit(solution)/shard_map/transpose | solution.py:500
  93.7 0.0 copy-done.7
  93.7 0.0 copy-done.5
  93.7 0.0 copy-done.8
  93.7 0.0 copy-done.4
  93.7 0.0 copy-done
  93.7 1.7 %rsqrt_multiply_fusion = f32[8,32,2048]{2,1,0:T(8,128)} fusion(f32[8,32,2048]{2,1,0:T(8,128)S(1)} %copy-done, f32[8]{0:T(128)S(1)} %broadcast_multiply_fusion, f32[8,2048]{1,0:T(8,128)S(1)} %get-tuple-element.49, f32[8,32]{1,0:T(8,128)S(1)} %get-tuple-element.48), kind=kLoop, calls=%fused_computation | loop fusion | flops 1572864 | bytes 4260896 | tf_op jit(solution)/shard_map/mul | solution.py:496
  95.4 0.8 copy.24
  96.2 0.8 copy.25
  (14 shorter events, 0.0 us)
Async XLA Ops:
  9.5 78.9 %copy-start.9 = (f32[8,32]{1,0:T(8,128)S(1)}, f32[8,32]{1,0:T(8,128)}, u32[]{:S(2)}) copy-start(f32[8,32]{1,0:T(8,128)} %param.23) | copy-start | bytes 3076
  9.5 78.9 %copy-start.10 = (f32[8,32]{1,0:T(8,128)S(1)}, f32[8,32]{1,0:T(8,128)}, u32[]{:S(2)}) copy-start(f32[8,32]{1,0:T(8,128)} %param.24) | copy-start | bytes 3076
  9.5 79.7 %copy-start.3 = (f32[8,2048]{1,0:T(8,128)S(1)}, f32[8,2048]{1,0:T(8,128)}, u32[]{:S(2)}) copy-start(f32[8,2048]{1,0:T(8,128)} %param.22) | copy-start | bytes 196612
  9.5 79.7 %copy-start.6 = (f32[8,2048]{1,0:T(8,128)S(1)}, f32[8,2048]{1,0:T(8,128)}, u32[]{:S(2)}) copy-start(f32[8,2048]{1,0:T(8,128)} %param.25) | copy-start | bytes 196612
  88.5 5.1 %copy-start.7 = (f32[8,32]{1,0:T(8,128)}, f32[8,32]{1,0:T(8,128)S(1)}, u32[]{:S(2)}) copy-start(f32[8,32]{1,0:T(8,128)S(1)} %get-tuple-element.47) | copy-start | bytes 3076
  88.5 5.1 %copy-start.8 = (f32[8,32]{1,0:T(8,128)}, f32[8,32]{1,0:T(8,128)S(1)}, u32[]{:S(2)}) copy-start(f32[8,32]{1,0:T(8,128)S(1)} %get-tuple-element.48) | copy-start | bytes 3076
  90.2 3.5 %copy-start.5 = (f32[8,2048]{1,0:T(8,128)}, f32[8,2048]{1,0:T(8,128)S(1)}, u32[]{:S(2)}) copy-start(f32[8,2048]{1,0:T(8,128)S(1)} %get-tuple-element.46) | copy-start | bytes 196612
  90.2 3.5 %copy-start.4 = (f32[8,2048]{1,0:T(8,128)}, f32[8,2048]{1,0:T(8,128)S(1)}, u32[]{:S(2)}) copy-start(f32[8,2048]{1,0:T(8,128)S(1)} %get-tuple-element.49) | copy-start | bytes 196612
  90.2 3.5 %copy-start = (f32[8,32,2048]{2,1,0:T(8,128)S(1)}, f32[8,32,2048]{2,1,0:T(8,128)}, u32[]{:S(2)}) copy-start(f32[8,32,2048]{2,1,0:T(8,128)} %get-tuple-element.20) | copy-start | bytes 6291460
  93.7 1.7 %copy-start.2 = (bf16[128,2048]{1,0:T(8,128)(2,1)S(1)}, bf16[128,2048]{1,0:T(8,128)(2,1)}, u32[]{:S(2)}) copy-start(bf16[128,2048]{1,0:T(8,128)(2,1)} %get-tuple-element.42) | copy-start | bytes 1572868
  93.7 2.5 %copy-start.1 = (bf16[2048,128]{1,0:T(8,128)(2,1)S(1)}, bf16[2048,128]{1,0:T(8,128)(2,1)}, u32[]{:S(2)}) copy-start(bf16[2048,128]{1,0:T(8,128)(2,1)} %get-tuple-element.43) | copy-start | bytes 1572868
